TPU v7x, 32 devices: a whole 2x2x4 slice. The times are simulated.
32 devices in a mesh: groups: 2 (over x), view: 16 (over z, y, core).
Axes of the slice: x: 2, y: 2, z: 4, core: 2. Of those that a mesh axis runs over, the one named last changes fastest.
Arguments:
- estimate: float32 [6144, 128], P(('groups', 'view')), parts along dimension 0, may hold values from 0.5 to 2, as said below
- measured: bfloat16 [512, 192, 128], P(('groups', 'view')), parts along dimension 0, may hold values from 0.25 to 4, as said below
- kernel_z: bfloat16 [16, 3, 128, 128], replicated, may hold values from 0 to 2, as said below
- kernel_x: bfloat16 [16, 3, 12, 12], replicated, may hold values from 0 to 2, as said below
- kernel_y: bfloat16 [16, 3, 16, 16], replicated, may hold values from 0 to 2, as said below
- background: bfloat16 [16], replicated, may hold values from 0.049804688 to 0.5
- relax: bfloat16 [16], replicated, may hold values from 0.029907227 to 0.23925781
- owner: int32 [512, 1], P(('groups', 'view')), parts along dimension 0, may hold values from 0 to 15; in each aligned block of 16 rows (0 to 15, 16 to 31, ...) at most 2 rows name the same one
- source_offset: int32 [512], P(('groups', 'view')), parts along dimension 0, may hold values from 0 to 184
- tile_offset: int32 [512], P(('groups', 'view')), parts along dimension 0, may hold values from 0 to 56
- feather: int32 [512, 8], P(('groups', 'view')), parts along dimension 0, may hold values from 1 to 8
Outputs:
- refined: float32 [6144, 128], P(('groups', 'view')), parts along dimension 0
- smoothed: float32 [2048, 128], P(('groups', 'view')), parts along dimension 0
There are 2 independent parts, one for each index of `groups`. A program takes and returns all parts, laid end to end along the dimension named above; an argument that names none is the same for every part. Nothing has to cross between parts.
Inputs may be any that keep to these rules, and one draw needn't show every extreme that they name: `owner`: within the 16 rows of one block no tile is named more than 2 times, and in every draw some tile is named exactly 2 times by some block. `kernel_z`: entries are nonnegative and every diagonal entry is positive. `kernel_x`: entries are nonnegative and every diagonal entry is positive. `kernel_y`: entries are nonnegative and every diagonal entry is positive. `estimate`: entries are positive. `measured`: entries are positive.
All inputs are finite; a program needn't handle non-finite values.
Results may differ from a plain program's by a relative error of at most 0.0006.
Values may be sent and summed in bfloat16 or wider, within the bound.
A program may use at most 64 MiB of HBM per device.

v0:
```python
import jax
import jax.numpy as jnp
from jax import lax
from jax.sharding import PartitionSpec as P

VIEWS = 16
SROWS = 8
TROWS = 64
CAP = 2


smooth_rate = 0.24
edge_scale = 1.0


def from_behind(block, axis, distance):
    devices = range(lax.axis_size(axis))
    route = [((i - distance) % len(devices), i) for i in devices]
    return lax.ppermute(block, axis, route)


def with_halo(block, sides, width):
    for axis, dim in sides:
        count = lax.axis_size(axis)
        forward = [(i, i + 1) for i in range(count - 1)]
        backward = [(target, source) for source, target in forward]
        low = lax.ppermute(
            lax.slice_in_dim(block, block.shape[dim] - width, None, axis=dim), axis, forward
        )
        high = lax.ppermute(lax.slice_in_dim(block, 0, width, axis=dim), axis, backward)
        block = jnp.concatenate([low, block, high], axis=dim)
    return block


def kron_rows(kernel_x, kernel_y):
    outer = (
        kernel_x.astype(jnp.float32)[..., :, None, :, None]
        * kernel_y.astype(jnp.float32)[..., None, :, None, :]
    )
    rows_xy = kernel_x.shape[-1] * kernel_y.shape[-1]
    return outer.reshape(outer.shape[:-4] + (rows_xy, rows_xy)).astype(jnp.bfloat16)


def visit_view(block, kernel_z, kernel_xy, measured_block, back_value, relax_value):
    lowered = block.astype(jnp.bfloat16)
    along_z = jnp.einsum(
        "iz,rkz->rik", lowered, kernel_z, preferred_element_type=jnp.float32
    ).astype(jnp.bfloat16)
    forward = jnp.einsum("rij,rjk->ik", kernel_xy, along_z, preferred_element_type=jnp.float32)
    ratio_lo = (measured_block.astype(jnp.float32) / (forward + back_value)).astype(jnp.bfloat16)
    back_z = jnp.einsum(
        "ik,rkz->riz", ratio_lo, kernel_z, preferred_element_type=jnp.float32
    ).astype(jnp.bfloat16)
    adjoint = jnp.einsum("rji,rjz->iz", kernel_xy, back_z, preferred_element_type=jnp.float32)
    column_xy = jnp.sum(kernel_xy.astype(jnp.float32), axis=1)
    column_z = jnp.sum(kernel_z.astype(jnp.float32), axis=1)
    weights_sum = jnp.einsum("ri,rz->iz", column_xy, column_z, precision=lax.Precision.HIGHEST)
    return block * jnp.exp(relax_value * jnp.log(adjoint / weights_sum))


def fetch_record(piece, offset):
    return from_behind(piece, "view", offset)


def on_device(
    estimate,
    measured,
    kernel_z,
    kernel_x,
    kernel_y,
    background,
    relax,
    owner,
    source_offset,
    tile_offset,
    feather,
):
    view_count = lax.axis_size("view")
    position = lax.axis_index("view")
    depth = estimate.shape[1]
    back_values = background.astype(jnp.float32)
    relax_values = relax.astype(jnp.float32)
    arrived = [measured[0]]
    for stop_id in range(1, VIEWS):
        arrived.append(fetch_record(measured[stop_id], -stop_id))
    records = jnp.stack(arrived, axis=0)

    def advance(stop_id, carried):
        view_id = (position + stop_id) % VIEWS
        kernel_xy = kron_rows(kernel_x[view_id], kernel_y[view_id])
        measured_block = lax.dynamic_index_in_dim(records, stop_id, 0, keepdims=False)
        return visit_view(
            carried,
            kernel_z[view_id],
            kernel_xy,
            measured_block,
            back_values[view_id],
            relax_values[view_id],
        )

    refined = lax.fori_loop(0, VIEWS, advance, estimate)
    listed = owner.shape[0]
    targets = owner[:, 0]
    window_rows = jnp.arange(SROWS, dtype=jnp.int32)
    sources = source_offset[:, None] + window_rows[None, :]
    weights = feather.astype(jnp.float32)
    pieces = refined[sources] * weights[..., None]
    entry_ids = jnp.arange(listed, dtype=jnp.int32)
    earlier = (targets[:, None] == targets[None, :]) & (entry_ids[None, :] < entry_ids[:, None])
    rank_in = jnp.sum(earlier.astype(jnp.int32), axis=1)
    slot_ids = targets * CAP + rank_in
    data_buf = (
        jnp.zeros((view_count * CAP, SROWS, depth), jnp.float32)
        .at[slot_ids]
        .set(pieces)
        .reshape(view_count, CAP, SROWS, depth)
    )
    weight_buf = (
        jnp.zeros((view_count * CAP, SROWS), jnp.float32)
        .at[slot_ids]
        .set(weights)
        .reshape(view_count, CAP, SROWS)
    )
    offset_buf = (
        jnp.zeros((view_count * CAP,), jnp.float32)
        .at[slot_ids]
        .set(tile_offset.astype(jnp.float32))
        .reshape(view_count, CAP)
    )
    data_in = lax.all_to_all(data_buf, "view", split_axis=0, concat_axis=0, tiled=True)
    weight_in = lax.all_to_all(weight_buf, "view", split_axis=0, concat_axis=0, tiled=True)
    offset_in = lax.all_to_all(offset_buf, "view", split_axis=0, concat_axis=0, tiled=True)
    tile_rows = jnp.arange(TROWS, dtype=jnp.float32)
    placed = (
        offset_in[:, :, None, None] + window_rows.astype(jnp.float32)[None, None, :, None]
        == tile_rows[None, None, None, :]
    ).astype(jnp.float32)
    summed = jnp.einsum("ncrt,ncrz->ctz", placed, data_in, precision=lax.Precision.HIGHEST)
    counted = jnp.einsum("ncrt,ncr->ct", placed, weight_in, precision=lax.Precision.HIGHEST)
    summed, counted = (summed, counted)
    numerator = 1.0 + jnp.sum(summed, axis=0)
    denominator = 1.0 + jnp.sum(counted, axis=0)
    joined = numerator / denominator[:, None]
    framed = with_halo(joined, (("view", 0),), 1)
    padded = jnp.pad(framed, ((0, 0), (1, 1)))
    flux_sum = jnp.zeros_like(joined)
    for neighbor in (padded[2:, 1:-1], padded[:-2, 1:-1], padded[1:-1, 2:], padded[1:-1, :-2]):
        change = neighbor - joined
        flux_sum = flux_sum + change / (1.0 + change / edge_scale * (change / edge_scale))
    smoothed = joined + smooth_rate * flux_sum
    return (refined, smoothed)


def solution(mesh):
    return jax.shard_map(
        on_device,
        mesh=mesh,
        in_specs=(
            P(("groups", "view"), None),
            P(("groups", "view"), None, None),
            P(),
            P(),
            P(),
            P(),
            P(),
            P(("groups", "view"), None),
            P(("groups", "view")),
            P(("groups", "view")),
            P(("groups", "view"), None),
        ),
        out_specs=(P(("groups", "view"), None), P(("groups", "view"), None)),
        check_vma=False,
    )
```

profile of v0, /device:TPU:0, one launch (start us, length us, event | category | flops | bytes accessed | tf_op | source)
XLA Modules:
  0.0 238.4 jit_solution(7790270060859869322)
XLA Ops:
  2.0 5.5 %collective-permute-start = (bf16[192,128]{1,0:T(8,128)(2,1)S(1)}, bf16[192,128]{1,0:T(8,128)(2,1)S(1)}, u32[]{:S(2)}, u32[]{:S(2)}) collective-permute-start(bf16[192,128]{1,0:T(8,128)(2,1)S(1)} %get-tuple-element.293), channel_id=1, source_target_pairs={{1,0},{2,1},{3,2},{4,3},{5,4},{6,5},{7,6},{8,7},{9,8},{10,9},{11,1... | collective-permute-start | bytes 147464 | tf_op jit(solution)/shard_map/ppermute | solution.py:19
  10.5 6.7 %all-to-all-start = ((f32[16,1,2]{2,1,0:T(1,128)}), f32[16,1,2]{2,1,0:T(1,128)S(1)}, u32[]{:S(2)}, u32[]{:S(2)}) async-start(f32[16,1,2]{2,1,0:T(1,128)} %bitcast.45), calls=%async_computation | async-start | bytes 16384 | tf_op jit(solution)/shard_map/all_to_all | solution.py:132
  18.8 4.8 %all-to-all-done = f32[16,1,2]{2,1,0:T(1,128)S(1)} async-done(((f32[16,1,2]{2,1,0:T(1,128)}), f32[16,1,2]{2,1,0:T(1,128)S(1)}, u32[]{:S(2)}, u32[]{:S(2)}) %all-to-all-start) | async-done | bytes 160 | tf_op jit(solution)/shard_map/all_to_all | solution.py:132
  23.6 3.5 %all-to-all-start.2 = ((f32[16,2,8]{2,1,0:T(2,128)}), f32[16,2,8]{2,1,0:T(2,128)S(1)}, u32[]{:S(2)}, u32[]{:S(2)}) async-start(f32[16,2,8]{2,1,0:T(2,128)} %bitcast.51), calls=%async_computation.2 | async-start | bytes 32768 | tf_op jit(solution)/shard_map/all_to_all | solution.py:131
  27.2 3.7 %collective-permute-start.5 = (bf16[192,128]{1,0:T(8,128)(2,1)S(1)}, bf16[192,128]{1,0:T(8,128)(2,1)S(1)}, u32[]{:S(2)}, u32[]{:S(2)}) collective-permute-start(bf16[192,128]{1,0:T(8,128)(2,1)S(1)} %get-tuple-element.288), channel_id=1, source_target_pairs={{6,0},{7,1},{8,2},{9,3},{10,4},{11,5},{12,6},{13,7},{14,8},{15,9},... | collective-permute-start | bytes 147464 | tf_op jit(solution)/shard_map/ppermute | solution.py:19
  30.9 2.4 %collective-permute-start.7 = (bf16[192,128]{1,0:T(8,128)(2,1)S(1)}, bf16[192,128]{1,0:T(8,128)(2,1)S(1)}, u32[]{:S(2)}, u32[]{:S(2)}) collective-permute-start(bf16[192,128]{1,0:T(8,128)(2,1)S(1)} %get-tuple-element.286), channel_id=1, source_target_pairs={{8,0},{9,1},{10,2},{11,3},{12,4},{13,5},{14,6},{15,7},{0,8},{1,9},... | collective-permute-start | bytes 147464 | tf_op jit(solution)/shard_map/ppermute | solution.py:19
  34.0 2.5 %collective-permute-start.9 = (bf16[192,128]{1,0:T(8,128)(2,1)S(1)}, bf16[192,128]{1,0:T(8,128)(2,1)S(1)}, u32[]{:S(2)}, u32[]{:S(2)}) collective-permute-start(bf16[192,128]{1,0:T(8,128)(2,1)S(1)} %get-tuple-element.284), channel_id=1, source_target_pairs={{10,0},{11,1},{12,2},{13,3},{14,4},{15,5},{0,6},{1,7},{2,8},{3,9},... | collective-permute-start | bytes 147464 | tf_op jit(solution)/shard_map/ppermute | solution.py:19
  37.4 2.0 collective-permute-start.11
  39.5 1.7 collective-permute-start.12
  42.6 2.6 %collective-permute-done.9 = bf16[192,128]{1,0:T(8,128)(2,1)S(1)} collective-permute-done((bf16[192,128]{1,0:T(8,128)(2,1)S(1)}, bf16[192,128]{1,0:T(8,128)(2,1)S(1)}, u32[]{:S(2)}, u32[]{:S(2)}) %collective-permute-start.9) | collective-permute-done | bytes 49184 | tf_op jit(solution)/shard_map/ppermute | solution.py:19
  45.3 1.5 collective-permute-done.10
  48.2 3.2 %collective-permute-done.14 = bf16[192,128]{1,0:T(8,128)(2,1)S(1)} collective-permute-done((bf16[192,128]{1,0:T(8,128)(2,1)S(1)}, bf16[192,128]{1,0:T(8,128)(2,1)S(1)}, u32[]{:S(2)}, u32[]{:S(2)}) %collective-permute-start.14) | collective-permute-done | bytes 49184 | tf_op jit(solution)/shard_map/ppermute | solution.py:19
  51.4 166.8 %while.15 = (s32[]{:T(128)}, f32[192,128]{1,0:T(8,128)S(1)}, s32[]{:T(128)}, f32[16]{0:T(128)S(1)}, bf16[16,3,12,12]{3,2,1,0:T(8,128)(2,1)S(1)}, /*index=5*/bf16...) while((s32[]{:T(128)}, f32[192,128]{1,0:T(8,128)S(1)}, ...), condition=%wide.region_3.4_spmd, body=%wide.region_0.3_spmd.sunk | while | flops 96141568 | bytes 8356960 | solution.py:101
  53.5 1.8 convert_element_type.219
  55.9 2.0 fusion.71
  63.9 1.8 convert_element_type.219
  66.4 2.0 fusion.71
  74.3 1.8 convert_element_type.219
  76.8 2.0 fusion.71
  84.8 1.8 convert_element_type.219
  87.2 2.0 fusion.71
  95.2 1.8 convert_element_type.219
  97.6 2.0 fusion.71
  105.6 1.8 convert_element_type.219
  108.0 2.0 fusion.71
  116.0 1.8 convert_element_type.219
  118.5 2.0 fusion.71
  126.4 1.8 convert_element_type.219
  128.9 2.0 fusion.71
  136.9 1.8 convert_element_type.219
  139.3 2.0 fusion.71
  147.3 1.8 convert_element_type.219
  149.7 2.0 fusion.71
  157.7 1.8 convert_element_type.219
  160.2 2.0 fusion.71
  168.1 1.8 convert_element_type.219
  170.6 2.0 fusion.71
  178.6 1.8 convert_element_type.219
  181.0 2.0 fusion.71
  189.0 1.8 convert_element_type.219
  191.4 2.0 fusion.71
  199.4 1.8 convert_element_type.219
  201.8 2.0 fusion.71
  209.8 1.8 convert_element_type.219
  212.3 2.0 fusion.71
  220.7 3.5 %all-to-all-start.1 = ((f32[16,2,8,128]{3,1,2,0:T(2,128)}), f32[16,2,8,128]{3,1,2,0:T(2,128)S(1)}, u32[]{:S(2)}, u32[]{:S(2)}) async-start(f32[16,2,8,128]{3,1,2,0:T(2,128)} %copy.36), calls=%async_computation.1 | async-start | bytes 262144 | tf_op jit(solution)/shard_map/all_to_all | solution.py:130
  224.6 7.5 %all-to-all-done.1 = f32[16,2,8,128]{3,1,2,0:T(2,128)S(1)} async-done(((f32[16,2,8,128]{3,1,2,0:T(2,128)}), f32[16,2,8,128]{3,1,2,0:T(2,128)S(1)}, u32[]{:S(2)}, u32[]{:S(2)}) %all-to-all-start.1) | async-done | bytes 131104 | tf_op jit(solution)/shard_map/all_to_all | solution.py:130
  233.7 3.0 %collective-permute-start.16 = (f32[1,128]{1,0:T(1,128)S(1)}, f32[1,128]{1,0:T(1,128)S(1)}, u32[]{:S(2)}, u32[]{:S(2)}) collective-permute-start(f32[1,128]{1,0:T(1,128)S(1)} %get-tuple-element.296), channel_id=1, source_target_pairs={{0,1},{1,2},{2,3},{3,4},{4,5},{5,6},{6,7},{7,8},{8,9},{9,10},{10,1... | collective-permute-start | bytes 1544 | tf_op jit(solution)/shard_map/ppermute | solution.py:27
  (295 shorter events, 120.9 us)
Async XLA Ops:
  0.6 16.8 %copy-start.2 = (bf16[16,3,12,12]{3,0,2,1:T(8,128)(2,1)S(1)}, bf16[16,3,12,12]{3,0,2,1:T(8,128)(2,1)}, u32[]{:S(2)}) copy-start(bf16[16,3,12,12]{3,0,2,1:T(8,128)(2,1)} %param.16) | copy-start | bytes 41476
  0.6 16.9 %copy-start.10 = (bf16[16]{0:T(256)(128)(2,1)S(1)}, bf16[16]{0:T(256)(128)(2,1)}, u32[]{:S(2)}) copy-start(bf16[16]{0:T(256)(128)(2,1)} %param.18) | copy-start | bytes 100
  0.7 16.8 %copy-start.9 = (bf16[16]{0:T(256)(128)(2,1)S(1)}, bf16[16]{0:T(256)(128)(2,1)}, u32[]{:S(2)}) copy-start(bf16[16]{0:T(256)(128)(2,1)} %param.19) | copy-start | bytes 100
  0.7 8.3 %copy-start.7 = (s32[16,1]{0,1:T(1,128)S(1)}, s32[16,1]{0,1:T(1,128)}, u32[]{:S(2)}) copy-start(s32[16,1]{0,1:T(1,128)} %param.20) | copy-start | bytes 196
  0.7 16.5 %copy-start.6 = (s32[16]{0:T(128)S(1)}, s32[16]{0:T(128)}, u32[]{:S(2)}) copy-start(s32[16]{0:T(128)} %param.21) | copy-start | bytes 196
  0.7 8.5 %copy-start.8 = (s32[16]{0:T(128)S(1)}, s32[16]{0:T(128)}, u32[]{:S(2)}) copy-start(s32[16]{0:T(128)} %param.22) | copy-start | bytes 196
  0.7 16.8 %copy-start.3 = (s32[16,8]{0,1:T(8,128)S(1)}, s32[16,8]{0,1:T(8,128)}, u32[]{:S(2)}) copy-start(s32[16,8]{0,1:T(8,128)} %param.23) | copy-start | bytes 1540
  0.7 50.7 %copy-start.1 = (f32[192,128]{1,0:T(8,128)S(1)}, f32[192,128]{1,0:T(8,128)}, u32[]{:S(2)}) copy-start(f32[192,128]{1,0:T(8,128)} %param.13) | copy-start | bytes 294916
  2.0 25.1 %collective-permute-start = (bf16[192,128]{1,0:T(8,128)(2,1)S(1)}, bf16[192,128]{1,0:T(8,128)(2,1)S(1)}, u32[]{:S(2)}, u32[]{:S(2)}) collective-permute-start(bf16[192,128]{1,0:T(8,128)(2,1)S(1)} %get-tuple-element.293), channel_id=1, source_target_pairs={{1,0},{2,1},{3,2},{4,3},{5,4},{6,5},{7,6},{8,7},{9,8},{10,9},{11,1... | collective-permute-start | bytes 147464 | tf_op jit(solution)/shard_map/ppermute | solution.py:19
  7.5 23.3 %collective-permute-start.1 = (bf16[192,128]{1,0:T(8,128)(2,1)S(1)}, bf16[192,128]{1,0:T(8,128)(2,1)S(1)}, u32[]{:S(2)}, u32[]{:S(2)}) collective-permute-start(bf16[192,128]{1,0:T(8,128)(2,1)S(1)} %get-tuple-element.292), channel_id=1, source_target_pairs={{2,0},{3,1},{4,2},{5,3},{6,4},{7,5},{8,6},{9,7},{10,8},{11,9},{12,... | collective-permute-start | bytes 147464 | tf_op jit(solution)/shard_map/ppermute | solution.py:19
  8.2 22.8 %collective-permute-start.2 = (bf16[192,128]{1,0:T(8,128)(2,1)S(1)}, bf16[192,128]{1,0:T(8,128)(2,1)S(1)}, u32[]{:S(2)}, u32[]{:S(2)}) collective-permute-start(bf16[192,128]{1,0:T(8,128)(2,1)S(1)} %get-tuple-element.291), channel_id=1, source_target_pairs={{3,0},{4,1},{5,2},{6,3},{7,4},{8,5},{9,6},{10,7},{11,8},{12,9},{13... | collective-permute-start | bytes 147464 | tf_op jit(solution)/shard_map/ppermute | solution.py:19
  8.4 25.0 %collective-permute-start.3 = (bf16[192,128]{1,0:T(8,128)(2,1)S(1)}, bf16[192,128]{1,0:T(8,128)(2,1)S(1)}, u32[]{:S(2)}, u32[]{:S(2)}) collective-permute-start(bf16[192,128]{1,0:T(8,128)(2,1)S(1)} %get-tuple-element.290), channel_id=1, source_target_pairs={{4,0},{5,1},{6,2},{7,3},{8,4},{9,5},{10,6},{11,7},{12,8},{13,9},{1... | collective-permute-start | bytes 147464 | tf_op jit(solution)/shard_map/ppermute | solution.py:19
  8.8 25.1 %collective-permute-start.4 = (bf16[192,128]{1,0:T(8,128)(2,1)S(1)}, bf16[192,128]{1,0:T(8,128)(2,1)S(1)}, u32[]{:S(2)}, u32[]{:S(2)}) collective-permute-start(bf16[192,128]{1,0:T(8,128)(2,1)S(1)} %get-tuple-element.289), channel_id=1, source_target_pairs={{5,0},{6,1},{7,2},{8,3},{9,4},{10,5},{11,6},{12,7},{13,8},{14,9},{... | collective-permute-start | bytes 147464 | tf_op jit(solution)/shard_map/ppermute | solution.py:19
  10.5 13.1 %all-to-all-start = ((f32[16,1,2]{2,1,0:T(1,128)}), f32[16,1,2]{2,1,0:T(1,128)S(1)}, u32[]{:S(2)}, u32[]{:S(2)}) async-start(f32[16,1,2]{2,1,0:T(1,128)} %bitcast.45), calls=%async_computation | async-start | bytes 16384 | tf_op jit(solution)/shard_map/all_to_all | solution.py:132
  23.6 197.1 %all-to-all-start.2 = ((f32[16,2,8]{2,1,0:T(2,128)}), f32[16,2,8]{2,1,0:T(2,128)S(1)}, u32[]{:S(2)}, u32[]{:S(2)}) async-start(f32[16,2,8]{2,1,0:T(2,128)} %bitcast.51), calls=%async_computation.2 | async-start | bytes 32768 | tf_op jit(solution)/shard_map/all_to_all | solution.py:131
  27.2 9.3 %collective-permute-start.5 = (bf16[192,128]{1,0:T(8,128)(2,1)S(1)}, bf16[192,128]{1,0:T(8,128)(2,1)S(1)}, u32[]{:S(2)}, u32[]{:S(2)}) collective-permute-start(bf16[192,128]{1,0:T(8,128)(2,1)S(1)} %get-tuple-element.288), channel_id=1, source_target_pairs={{6,0},{7,1},{8,2},{9,3},{10,4},{11,5},{12,6},{13,7},{14,8},{15,9},... | collective-permute-start | bytes 147464 | tf_op jit(solution)/shard_map/ppermute | solution.py:19
  30.8 6.6 %collective-permute-start.6 = (bf16[192,128]{1,0:T(8,128)(2,1)S(1)}, bf16[192,128]{1,0:T(8,128)(2,1)S(1)}, u32[]{:S(2)}, u32[]{:S(2)}) collective-permute-start(bf16[192,128]{1,0:T(8,128)(2,1)S(1)} %get-tuple-element.287), channel_id=1, source_target_pairs={{7,0},{8,1},{9,2},{10,3},{11,4},{12,5},{13,6},{14,7},{15,8},{0,9},... | collective-permute-start | bytes 147464 | tf_op jit(solution)/shard_map/ppermute | solution.py:19
  30.9 8.5 %collective-permute-start.7 = (bf16[192,128]{1,0:T(8,128)(2,1)S(1)}, bf16[192,128]{1,0:T(8,128)(2,1)S(1)}, u32[]{:S(2)}, u32[]{:S(2)}) collective-permute-start(bf16[192,128]{1,0:T(8,128)(2,1)S(1)} %get-tuple-element.286), channel_id=1, source_target_pairs={{8,0},{9,1},{10,2},{11,3},{12,4},{13,5},{14,6},{15,7},{0,8},{1,9},... | collective-permute-start | bytes 147464 | tf_op jit(solution)/shard_map/ppermute | solution.py:19
  33.4 7.8 %collective-permute-start.8 = (bf16[192,128]{1,0:T(8,128)(2,1)S(1)}, bf16[192,128]{1,0:T(8,128)(2,1)S(1)}, u32[]{:S(2)}, u32[]{:S(2)}) collective-permute-start(bf16[192,128]{1,0:T(8,128)(2,1)S(1)} %get-tuple-element.285), channel_id=1, source_target_pairs={{9,0},{10,1},{11,2},{12,3},{13,4},{14,5},{15,6},{0,7},{1,8},{2,9},... | collective-permute-start | bytes 147464 | tf_op jit(solution)/shard_map/ppermute | solution.py:19
  34.0 11.2 %collective-permute-start.9 = (bf16[192,128]{1,0:T(8,128)(2,1)S(1)}, bf16[192,128]{1,0:T(8,128)(2,1)S(1)}, u32[]{:S(2)}, u32[]{:S(2)}) collective-permute-start(bf16[192,128]{1,0:T(8,128)(2,1)S(1)} %get-tuple-element.284), channel_id=1, source_target_pairs={{10,0},{11,1},{12,2},{13,3},{14,4},{15,5},{0,6},{1,7},{2,8},{3,9},... | collective-permute-start | bytes 147464 | tf_op jit(solution)/shard_map/ppermute | solution.py:19
  36.4 10.3 %collective-permute-start.10 = (bf16[192,128]{1,0:T(8,128)(2,1)S(1)}, bf16[192,128]{1,0:T(8,128)(2,1)S(1)}, u32[]{:S(2)}, u32[]{:S(2)}) collective-permute-start(bf16[192,128]{1,0:T(8,128)(2,1)S(1)} %get-tuple-element.283), channel_id=1, source_target_pairs={{11,0},{12,1},{13,2},{14,3},{15,4},{0,5},{1,6},{2,7},{3,8},{4,9},{... | collective-permute-start | bytes 147464 | tf_op jit(solution)/shard_map/ppermute | solution.py:19
  37.4 9.3 %collective-permute-start.11 = (bf16[192,128]{1,0:T(8,128)(2,1)S(1)}, bf16[192,128]{1,0:T(8,128)(2,1)S(1)}, u32[]{:S(2)}, u32[]{:S(2)}) collective-permute-start(bf16[192,128]{1,0:T(8,128)(2,1)S(1)} %get-tuple-element.282), channel_id=1, source_target_pairs={{12,0},{13,1},{14,2},{15,3},{0,4},{1,5},{2,6},{3,7},{4,8},{5,9},{6... | collective-permute-start | bytes 147464 | tf_op jit(solution)/shard_map/ppermute | solution.py:19
  39.5 7.4 %collective-permute-start.12 = (bf16[192,128]{1,0:T(8,128)(2,1)S(1)}, bf16[192,128]{1,0:T(8,128)(2,1)S(1)}, u32[]{:S(2)}, u32[]{:S(2)}) collective-permute-start(bf16[192,128]{1,0:T(8,128)(2,1)S(1)} %get-tuple-element.281), channel_id=1, source_target_pairs={{13,0},{14,1},{15,2},{0,3},{1,4},{2,5},{3,6},{4,7},{5,8},{6,9},{7,... | collective-permute-start | bytes 147464 | tf_op jit(solution)/shard_map/ppermute | solution.py:19
  41.1 7.1 %collective-permute-start.13 = (bf16[192,128]{1,0:T(8,128)(2,1)S(1)}, bf16[192,128]{1,0:T(8,128)(2,1)S(1)}, u32[]{:S(2)}, u32[]{:S(2)}) collective-permute-start(bf16[192,128]{1,0:T(8,128)(2,1)S(1)} %get-tuple-element.295), channel_id=1, source_target_pairs={{14,0},{15,1},{0,2},{1,3},{2,4},{3,5},{4,6},{5,7},{6,8},{7,9},{8,1... | collective-permute-start | bytes 147464 | tf_op jit(solution)/shard_map/ppermute | solution.py:19
  45.2 6.2 %collective-permute-start.14 = (bf16[192,128]{1,0:T(8,128)(2,1)S(1)}, bf16[192,128]{1,0:T(8,128)(2,1)S(1)}, u32[]{:S(2)}, u32[]{:S(2)}) collective-permute-start(bf16[192,128]{1,0:T(8,128)(2,1)S(1)} %get-tuple-element.280), channel_id=1, source_target_pairs={{15,0},{0,1},{1,2},{2,3},{3,4},{4,5},{5,6},{6,7},{7,8},{8,9},{9,10... | collective-permute-start | bytes 147464 | tf_op jit(solution)/shard_map/ppermute | solution.py:19
  51.4 0.9 copy-start.4
  55.3 6.5 %copy-start.5 = (bf16[16,192,128]{2,1,0:T(8,128)(2,1)S(1)}, bf16[16,192,128]{2,1,0:T(8,128)(2,1)}, u32[]{:S(2)}) copy-start(bf16[16,192,128]{2,1,0:T(8,128)(2,1)} %copy-done.4) | copy-start | bytes 2359300 | tf_op jit(solution)/shard_map/while
  65.8 6.5 %copy-start.5 = (bf16[16,192,128]{2,1,0:T(8,128)(2,1)S(1)}, bf16[16,192,128]{2,1,0:T(8,128)(2,1)}, u32[]{:S(2)}) copy-start(bf16[16,192,128]{2,1,0:T(8,128)(2,1)} %copy-done.4) | copy-start | bytes 2359300 | tf_op jit(solution)/shard_map/while
  76.2 6.5 %copy-start.5 = (bf16[16,192,128]{2,1,0:T(8,128)(2,1)S(1)}, bf16[16,192,128]{2,1,0:T(8,128)(2,1)}, u32[]{:S(2)}) copy-start(bf16[16,192,128]{2,1,0:T(8,128)(2,1)} %copy-done.4) | copy-start | bytes 2359300 | tf_op jit(solution)/shard_map/while
  82.7 0.9 copy-start.4
  86.6 6.5 %copy-start.5 = (bf16[16,192,128]{2,1,0:T(8,128)(2,1)S(1)}, bf16[16,192,128]{2,1,0:T(8,128)(2,1)}, u32[]{:S(2)}) copy-start(bf16[16,192,128]{2,1,0:T(8,128)(2,1)} %copy-done.4) | copy-start | bytes 2359300 | tf_op jit(solution)/shard_map/while
  97.0 6.5 %copy-start.5 = (bf16[16,192,128]{2,1,0:T(8,128)(2,1)S(1)}, bf16[16,192,128]{2,1,0:T(8,128)(2,1)}, u32[]{:S(2)}) copy-start(bf16[16,192,128]{2,1,0:T(8,128)(2,1)} %copy-done.4) | copy-start | bytes 2359300 | tf_op jit(solution)/shard_map/while
  107.4 6.5 %copy-start.5 = (bf16[16,192,128]{2,1,0:T(8,128)(2,1)S(1)}, bf16[16,192,128]{2,1,0:T(8,128)(2,1)}, u32[]{:S(2)}) copy-start(bf16[16,192,128]{2,1,0:T(8,128)(2,1)} %copy-done.4) | copy-start | bytes 2359300 | tf_op jit(solution)/shard_map/while
  117.9 6.5 %copy-start.5 = (bf16[16,192,128]{2,1,0:T(8,128)(2,1)S(1)}, bf16[16,192,128]{2,1,0:T(8,128)(2,1)}, u32[]{:S(2)}) copy-start(bf16[16,192,128]{2,1,0:T(8,128)(2,1)} %copy-done.4) | copy-start | bytes 2359300 | tf_op jit(solution)/shard_map/while
  128.3 6.5 %copy-start.5 = (bf16[16,192,128]{2,1,0:T(8,128)(2,1)S(1)}, bf16[16,192,128]{2,1,0:T(8,128)(2,1)}, u32[]{:S(2)}) copy-start(bf16[16,192,128]{2,1,0:T(8,128)(2,1)} %copy-done.4) | copy-start | bytes 2359300 | tf_op jit(solution)/shard_map/while
  134.8 0.9 copy-start.4
  138.7 6.5 %copy-start.5 = (bf16[16,192,128]{2,1,0:T(8,128)(2,1)S(1)}, bf16[16,192,128]{2,1,0:T(8,128)(2,1)}, u32[]{:S(2)}) copy-start(bf16[16,192,128]{2,1,0:T(8,128)(2,1)} %copy-done.4) | copy-start | bytes 2359300 | tf_op jit(solution)/shard_map/while
  149.1 6.5 %copy-start.5 = (bf16[16,192,128]{2,1,0:T(8,128)(2,1)S(1)}, bf16[16,192,128]{2,1,0:T(8,128)(2,1)}, u32[]{:S(2)}) copy-start(bf16[16,192,128]{2,1,0:T(8,128)(2,1)} %copy-done.4) | copy-start | bytes 2359300 | tf_op jit(solution)/shard_map/while
  159.6 6.5 %copy-start.5 = (bf16[16,192,128]{2,1,0:T(8,128)(2,1)S(1)}, bf16[16,192,128]{2,1,0:T(8,128)(2,1)}, u32[]{:S(2)}) copy-start(bf16[16,192,128]{2,1,0:T(8,128)(2,1)} %copy-done.4) | copy-start | bytes 2359300 | tf_op jit(solution)/shard_map/while
  170.0 6.5 %copy-start.5 = (bf16[16,192,128]{2,1,0:T(8,128)(2,1)S(1)}, bf16[16,192,128]{2,1,0:T(8,128)(2,1)}, u32[]{:S(2)}) copy-start(bf16[16,192,128]{2,1,0:T(8,128)(2,1)} %copy-done.4) | copy-start | bytes 2359300 | tf_op jit(solution)/shard_map/while
  180.4 6.5 %copy-start.5 = (bf16[16,192,128]{2,1,0:T(8,128)(2,1)S(1)}, bf16[16,192,128]{2,1,0:T(8,128)(2,1)}, u32[]{:S(2)}) copy-start(bf16[16,192,128]{2,1,0:T(8,128)(2,1)} %copy-done.4) | copy-start | bytes 2359300 | tf_op jit(solution)/shard_map/while
  190.8 6.5 %copy-start.5 = (bf16[16,192,128]{2,1,0:T(8,128)(2,1)S(1)}, bf16[16,192,128]{2,1,0:T(8,128)(2,1)}, u32[]{:S(2)}) copy-start(bf16[16,192,128]{2,1,0:T(8,128)(2,1)} %copy-done.4) | copy-start | bytes 2359300 | tf_op jit(solution)/shard_map/while
  201.2 6.5 %copy-start.5 = (bf16[16,192,128]{2,1,0:T(8,128)(2,1)S(1)}, bf16[16,192,128]{2,1,0:T(8,128)(2,1)}, u32[]{:S(2)}) copy-start(bf16[16,192,128]{2,1,0:T(8,128)(2,1)} %copy-done.4) | copy-start | bytes 2359300 | tf_op jit(solution)/shard_map/while
  211.7 6.5 %copy-start.5 = (bf16[16,192,128]{2,1,0:T(8,128)(2,1)S(1)}, bf16[16,192,128]{2,1,0:T(8,128)(2,1)}, u32[]{:S(2)}) copy-start(bf16[16,192,128]{2,1,0:T(8,128)(2,1)} %copy-done.4) | copy-start | bytes 2359300 | tf_op jit(solution)/shard_map/while
  218.2 20.2 %copy-start = (f32[192,128]{1,0:T(8,128)}, f32[192,128]{1,0:T(8,128)S(1)}, u32[]{:S(2)}) copy-start(f32[192,128]{1,0:T(8,128)S(1)} %get-tuple-element.221) | copy-start | bytes 294916
  220.7 11.4 %all-to-all-start.1 = ((f32[16,2,8,128]{3,1,2,0:T(2,128)}), f32[16,2,8,128]{3,1,2,0:T(2,128)S(1)}, u32[]{:S(2)}, u32[]{:S(2)}) async-start(f32[16,2,8,128]{3,1,2,0:T(2,128)} %copy.36), calls=%async_computation.1 | async-start | bytes 262144 | tf_op jit(solution)/shard_map/all_to_all | solution.py:130
  232.4 4.3 %collective-permute-start.15 = (f32[1,128]{1,0:T(1,128)S(1)}, f32[1,128]{1,0:T(1,128)S(1)}, u32[]{:S(2)}, u32[]{:S(2)}) collective-permute-start(f32[1,128]{1,0:T(1,128)S(1)} %get-tuple-element.297), channel_id=1, source_target_pairs={{1,0},{2,1},{3,2},{4,3},{5,4},{6,5},{7,6},{8,7},{9,8},{10,9},{11,1... | collective-permute-start | bytes 1544 | tf_op jit(solution)/shard_map/ppermute | solution.py:30
  233.7 3.8 %collective-permute-start.16 = (f32[1,128]{1,0:T(1,128)S(1)}, f32[1,128]{1,0:T(1,128)S(1)}, u32[]{:S(2)}, u32[]{:S(2)}) collective-permute-start(f32[1,128]{1,0:T(1,128)S(1)} %get-tuple-element.296), channel_id=1, source_target_pairs={{0,1},{1,2},{2,3},{3,4},{4,5},{5,6},{6,7},{7,8},{8,9},{9,10},{10,1... | collective-permute-start | bytes 1544 | tf_op jit(solution)/shard_map/ppermute | solution.py:27
  (13 other events, 11.5 us)
where the time goes:
time: 242 us; the launch traced here: 238 us
  matrix products  69.3 us (29%)
  local copies, waits for them, and re-layouts  58.2 us (24%)
  other arithmetic  46.3 us (19%)
  starting transfers between devices  40.3 us (17%)
  waiting for transfers between devices  21.7 us (9%)
    dot_general x16, matrix products, visit_view(): jnp.einsum('rij,rjk->ik', kernel_xy, along_z, preferred_element_type=jnp....  31.5 us
    convert_element_type x16, local copies, waits for them, and re-layouts, kron_rows(): outer.reshape(outer.shape[:-4] + (rows_xy, rows_xy)).astype(jnp.bfloat16)  29.4 us
    ppermute x15, starting transfers between devices, from_behind(): return lax.ppermute(block, axis, route)  22.3 us
    dot_general x16, matrix products, visit_view(): jnp.einsum('rji,rjz->iz', kernel_xy, back_z, preferred_element_type=jnp.f...  20.8 us
    reduce_sum x16, other arithmetic, visit_view(): column_xy = jnp.sum(kernel_xy.astype(jnp.float32), axis=1)  18.3 us
    dot_general x16, matrix products, visit_view(): jnp.einsum('ri,rz->iz', column_xy, column_z, precision=lax.Precision.HIGH...  16.4 us
    reduce_sum x16, other arithmetic, visit_view(): column_z = jnp.sum(kernel_z.astype(jnp.float32), axis=1)  14.8 us
    convert_element_type x16, other arithmetic, kron_rows(): kernel_y.astype(jnp.float32)[..., None, :, None, :]  11.9 us
  transfers between devices with their start and end apart: 20, of which 7 were waited for; matrix products, arithmetic and copies ran while one was open for 71% of the time, Pallas kernels for 0%

commit v1 on v0

v1 whole, which is shorter than its diff:
```python
import functools

import jax
import jax.numpy as jnp
import numpy as np
from jax import lax
from jax.experimental import pallas as pl
from jax.experimental.pallas import tpu as pltpu
from jax.sharding import PartitionSpec as P

CAP = 2
TROWS = 64
smooth_rate = 0.24

f32 = jnp.float32
bf16 = jnp.bfloat16


def split3(x):
    hi = x.astype(bf16)
    rest = x - hi.astype(f32)
    mid = rest.astype(bf16)
    low = (rest - mid.astype(f32)).astype(bf16)
    return hi, mid, low


def onehot_dot(onehot, parts):
    total = None
    for part in reversed(parts):
        term = jnp.dot(onehot, part, preferred_element_type=f32)
        total = term if total is None else total + term
    return total


def kernel(
    nv,
    views,
    bx,
    by,
    srows,
    scal_ref,
    est_ref,
    meas_hbm,
    kz_hbm,
    fac_ref,
    sel_ref,
    owner_ref,
    meta_ref,
    refined_ref,
    smooth_ref,
    rec,
    kz,
    lanes,
    kron,
    logws,
    meta_send,
    meta_recv,
    gather,
    wcol,
    place,
    data_send,
    data_recv,
    joined_ref,
    halo,
    rec_send_sem,
    rec_recv_sem,
    kz_sem,
    meta_send_sem,
    meta_recv_sem,
    data_send_sem,
    data_recv_sem,
    halo_send_sem,
    halo_recv_sem,
):
    me = lax.axis_index("view")
    rows, depth = est_ref.shape
    rank = kz.shape[1]
    listed = owner_ref.shape[0]
    slab = CAP * srows
    landing = nv * slab

    barrier = pltpu.get_barrier_semaphore()

    def greet(d, c):
        pl.semaphore_signal(barrier, inc=1, device_id={"view": lax.rem(me + d, nv)})
        return c

    lax.fori_loop(1, nv, greet, 0)

    own_rec = pltpu.make_async_copy(meas_hbm.at[0], rec.at[0], rec_recv_sem.at[0])
    own_rec.start()
    kz_copy = pltpu.make_async_copy(kz_hbm, kz, kz_sem)
    kz_copy.start()

    def rec_copy(s):
        return pltpu.make_async_remote_copy(
            src_ref=meas_hbm.at[s],
            dst_ref=rec.at[s],
            send_sem=rec_send_sem.at[s],
            recv_sem=rec_recv_sem.at[s],
            device_id={"view": lax.rem(me - s + nv, nv)},
        )

    def peer_copy(src, dst, send_sem, recv_sem, d):
        peer = lax.rem(me + d, nv)
        return pltpu.make_async_remote_copy(
            src_ref=src.at[peer],
            dst_ref=dst.at[me],
            send_sem=send_sem.at[d],
            recv_sem=recv_sem.at[d],
            device_id={"view": peer},
        )

    def meta_copy(d):
        return peer_copy(meta_send, meta_recv, meta_send_sem, meta_recv_sem, d)

    def data_copy(d):
        return peer_copy(data_send, data_recv, data_send_sem, data_recv_sem, d)

    own_col = owner_ref[...].astype(f32)
    own_wide = jnp.broadcast_to(own_col, (listed, 128))
    if listed < 128:
        own_wide = jnp.concatenate([own_wide, jnp.full((128 - listed, 128), -1.0, f32)], axis=0)
    own_row = own_wide.T[0:1, :]
    same = (own_wide == own_row).astype(f32)
    ia = lax.broadcasted_iota(jnp.int32, (128, 128), 0)
    ib = lax.broadcasted_iota(jnp.int32, (128, 128), 1)
    earlier = jnp.where(ia < ib, same, 0.0)
    rank_row = jnp.sum(earlier, axis=0, keepdims=True)
    slot_row = own_row * CAP + rank_row
    slot_of_row = (lax.broadcasted_iota(jnp.int32, (landing, 128), 0) >> 3).astype(f32)
    pick = (slot_of_row == slot_row).astype(f32)[:, :listed].astype(bf16)
    meta = jnp.dot(pick, meta_ref[...].astype(bf16), preferred_element_type=f32)
    meta_send[...] = meta.reshape(nv, slab, 128)

    view0 = lax.rem(me, views)

    def expand(view, slot):
        lanes[...] = jnp.dot(fac_ref[view], sel_ref[...], preferred_element_type=f32)
        for t in range(2):
            base = t * 2 * 16
            y_part = lanes[base + 16 : base + 16 + by, :]
            for x in range(bx):
                x_part = lanes[base + x : base + x + 1, :]
                kron[slot, t, x * by : (x + 1) * by, :] = (x_part * y_part).astype(bf16)

    def weigh(view, slot):
        pieces = []
        for r in range(rank):
            column = jnp.sum(kz[view, r].astype(f32), axis=0, keepdims=True)
            hi = column.astype(bf16).astype(f32)
            both = jnp.concatenate([hi, column - hi], axis=1)
            pieces.append(jnp.broadcast_to(both, (rows, 2 * depth)).astype(bf16))
        halves = jnp.dot(kron[slot, 1], jnp.concatenate(pieces, axis=0), preferred_element_type=f32)
        logws[slot] = jnp.log(halves[:, :depth] + halves[:, depth:])

    expand(view0, 0)
    pl.semaphore_wait(barrier, nv - 1)

    def send_rec(s, c):
        rec_copy(s).start()
        return c

    lax.fori_loop(1, views, send_rec, 0)

    def send_meta(d, c):
        meta_copy(d).start()
        return c

    lax.fori_loop(1, nv, send_meta, 0)

    refined_ref[...] = est_ref[...]
    kz_copy.wait()
    weigh(view0, 0)
    q_of_row = (lax.broadcasted_iota(jnp.int32, (landing, 128), 0) & 7).astype(f32)
    lane_of = lax.broadcasted_iota(jnp.int32, (landing, 128), 1).astype(f32)
    valid = meta[:, 2:3]
    source = meta[:, 0:1] + q_of_row[:, 0:1] + (valid - 1.0) * 4096.0
    lane_rows = lax.broadcasted_iota(jnp.int32, (landing, rows), 1).astype(f32)
    gather[...] = (lane_rows == source).astype(f32).astype(bf16)
    wcol[...] = jnp.broadcast_to(
        jnp.sum(jnp.where(lane_of == q_of_row + 3.0, meta, 0.0), axis=1, keepdims=True), (landing, depth)
    )
    own_rec.wait()

    def stop(s, c):
        @pl.when(s > 0)
        def _():
            rec_copy(s).wait_recv()

        slot = lax.rem(s, 2)
        view = lax.rem(me + s, views)
        e = refined_ref[...]
        zeta = kz[view]
        low = e.astype(bf16)
        along = [
            lax.dot_general(
                low, zeta[r], (((1,), (1,)), ((), ())), preferred_element_type=f32
            ).astype(bf16)
            for r in range(rank)
        ]
        forward = jnp.dot(kron[slot, 0], jnp.concatenate(along, axis=0), preferred_element_type=f32)
        ratio = (rec[s].astype(f32) / (forward + scal_ref[0, view])).astype(bf16)
        back = [
            jnp.dot(ratio, zeta[r], preferred_element_type=f32).astype(bf16) for r in range(rank)
        ]
        adjoint = jnp.dot(kron[slot, 1], jnp.concatenate(back, axis=0), preferred_element_type=f32)
        refined_ref[...] = e * jnp.exp(scal_ref[1, view] * (jnp.log(adjoint) - logws[slot]))
        following = lax.rem(view + 1, views)
        expand(following, 1 - slot)
        weigh(following, 1 - slot)
        return c

    lax.fori_loop(0, views, stop, 0)

    refined = refined_ref[...]
    lines = onehot_dot(gather[...], split3(refined)) * wcol[...]
    data_send[...] = lines.reshape(nv, slab, depth)

    def send_data(d, c):
        data_copy(d).start()
        return c

    lax.fori_loop(1, nv, send_data, 0)
    data_recv[me] = data_send[me]
    meta_recv[me] = meta_send[me]

    def take_meta(d, c):
        meta_copy(d).wait()
        return c

    lax.fori_loop(1, nv, take_meta, 0)

    def done_rec(s, c):
        rec_copy(s).wait_send()
        return c

    lax.fori_loop(1, views, done_rec, 0)

    arrived = meta_recv[...].reshape(landing, 128)
    target = arrived[:, 1:2] + q_of_row[:, 0:1] + (arrived[:, 2:3] - 1.0) * 4096.0
    place_t = (lane_of == target).astype(f32)
    placed = place_t.T[0:TROWS, :].astype(bf16)
    weights = jnp.sum(jnp.where(lane_of == q_of_row + 3.0, arrived, 0.0), axis=1, keepdims=True)
    counted = jnp.dot(
        placed, jnp.broadcast_to(weights, (landing, depth)).astype(bf16), preferred_element_type=f32
    )

    def take_data(d, c):
        data_copy(d).wait()
        return c

    lax.fori_loop(1, nv, take_data, 0)
    summed = onehot_dot(placed, split3(data_recv[...].reshape(landing, depth)))
    joined = (1.0 + summed) / (1.0 + counted)
    joined_ref[...] = joined

    up_copy = pltpu.make_async_remote_copy(
        src_ref=joined_ref.at[pl.ds(TROWS - 8, 8)],
        dst_ref=halo.at[0],
        send_sem=halo_send_sem.at[0],
        recv_sem=halo_recv_sem.at[0],
        device_id={"view": lax.rem(me + 1, nv)},
    )
    down_copy = pltpu.make_async_remote_copy(
        src_ref=joined_ref.at[pl.ds(0, 8)],
        dst_ref=halo.at[1],
        send_sem=halo_send_sem.at[1],
        recv_sem=halo_recv_sem.at[1],
        device_id={"view": lax.rem(me - 1 + nv, nv)},
    )
    up_copy.start()
    down_copy.start()

    lane = lax.broadcasted_iota(jnp.int32, (TROWS, depth), 1)
    line = lax.broadcasted_iota(jnp.int32, (TROWS, depth), 0)

    def flux(neighbor):
        change = neighbor - joined
        return change / (1.0 + change * change)

    right = jnp.where(lane == depth - 1, 0.0, pltpu.roll(joined, depth - 1, 1))
    left = jnp.where(lane == 0, 0.0, pltpu.roll(joined, 1, 1))
    along_depth = flux(right) + flux(left)
    after = pltpu.roll(joined, TROWS - 1, 0)
    before = pltpu.roll(joined, 1, 0)
    up_copy.wait()
    down_copy.wait()
    has_low = (me > 0).astype(f32)
    has_high = (me < nv - 1).astype(f32)
    low_line = halo[0, 7:8, :] * has_low
    high_line = halo[1, 0:1, :] * has_high
    after = jnp.where(line == TROWS - 1, high_line, after)
    before = jnp.where(line == 0, low_line, before)
    smooth_ref[...] = joined + smooth_rate * (flux(after) + flux(before) + along_depth)


def on_device(
    estimate,
    measured,
    kernel_z,
    kernel_x,
    kernel_y,
    background,
    relax,
    owner,
    source_offset,
    tile_offset,
    feather,
):
    nv = lax.axis_size("view")
    views, rank, bx, _ = kernel_x.shape
    by = kernel_y.shape[-1]
    rows, depth = estimate.shape
    srows = feather.shape[1]
    listed = owner.shape[0]
    slab = CAP * srows
    landing = nv * slab

    scal = jnp.stack([background.astype(f32), relax.astype(f32)])

    def facts(factor, extent, before, after):
        both = jnp.stack(
            [factor.transpose(0, 2, 1, 3), factor.transpose(0, 3, 1, 2)], axis=1
        ).reshape(views, 2, extent, rank * extent)
        return jnp.pad(both, ((0, 0), (0, 0), (0, 16 - extent), (before, after)))

    fac = jnp.stack(
        [facts(kernel_x, bx, 0, rank * by), facts(kernel_y, by, rank * bx, 0)], axis=2
    ).reshape(views, 64, rank * (bx + by))
    col = np.arange(rank * rows)
    sel_x = col[None, :] // by == np.arange(rank * bx)[:, None]
    sel_y = (col // rows * by + col % by)[None, :] == np.arange(rank * by)[:, None]
    sel = jnp.asarray(np.concatenate([sel_x, sel_y]).astype(np.float32), bf16)
    meta = jnp.concatenate(
        [
            source_offset[:, None],
            tile_offset[:, None],
            jnp.ones((listed, 1), jnp.int32),
            feather,
            jnp.zeros((listed, 128 - 3 - srows), jnp.int32),
        ],
        axis=1,
    ).astype(f32)

    vmem = pl.BlockSpec(memory_space=pltpu.VMEM)
    anym = pl.BlockSpec(memory_space=pl.ANY)
    dma = pltpu.SemaphoreType.DMA
    return pl.pallas_call(
        functools.partial(kernel, nv, views, bx, by, srows),
        out_shape=(
            jax.ShapeDtypeStruct((rows, depth), f32),
            jax.ShapeDtypeStruct((TROWS, depth), f32),
        ),
        in_specs=[
            pl.BlockSpec(memory_space=pltpu.SMEM),
            vmem,
            anym,
            anym,
            vmem,
            vmem,
            vmem,
            vmem,
        ],
        out_specs=(vmem, vmem),
        scratch_shapes=[
            pltpu.VMEM((views, rows, depth), bf16),
            pltpu.VMEM(kernel_z.shape, bf16),
            pltpu.VMEM((64, rank * rows), f32),
            pltpu.VMEM((2, 2, rows, rank * rows), bf16),
            pltpu.VMEM((2, rows, depth), f32),
            pltpu.VMEM((nv, slab, 128), f32),
            pltpu.VMEM((nv, slab, 128), f32),
            pltpu.VMEM((landing, rows), bf16),
            pltpu.VMEM((landing, depth), f32),
            pltpu.VMEM((TROWS, landing), bf16),
            pltpu.VMEM((nv, slab, depth), f32),
            pltpu.VMEM((nv, slab, depth), f32),
            pltpu.VMEM((TROWS, depth), f32),
            pltpu.VMEM((2, 8, depth), f32),
            dma((views,)),
            dma((views,)),
            dma,
            dma((nv,)),
            dma((nv,)),
            dma((nv,)),
            dma((nv,)),
            dma((2,)),
            dma((2,)),
        ],
        compiler_params=pltpu.CompilerParams(collective_id=0, has_side_effects=True),
    )(scal, estimate, measured, kernel_z, fac, sel, owner, meta)


def solution(mesh):
    return jax.shard_map(
        on_device,
        mesh=mesh,
        in_specs=(
            P(("groups", "view"), None),
            P(("groups", "view"), None, None),
            P(),
            P(),
            P(),
            P(),
            P(),
            P(("groups", "view"), None),
            P(("groups", "view")),
            P(("groups", "view")),
            P(("groups", "view"), None),
        ),
        out_specs=(P(("groups", "view"), None), P(("groups", "view"), None)),
        check_vma=False,
    )
```

time: 242 us -> 58.9 us (0.24); the launches traced: 238 us -> 58.6 us
  matrix products: 69.3 us -> 0 us
  local copies, waits for them, and re-layouts: 58.2 us -> 8.45 us
  Pallas kernels: 0 us -> 48.1 us
  other arithmetic: 46.3 us -> 1.33 us
  starting transfers between devices: 40.3 us -> 0 us
  waiting for transfers between devices: 21.7 us -> 0 us
    dot_general x50 -> x0, matrix products: 69.3 us -> none  [the longest x16 31.5 us: visit_view(): jnp.einsum('rij,rjk->ik', kernel_xy, along_z, preferred_element_type=jnp....]
    pallas_call x0 -> x1, Pallas kernels: none -> 48.1 us  [on_device(): pl.pallas_call(functools.partial(kernel, nv, views, bx, by, srows), out_s...]
    reduce_sum x33 -> x0, other arithmetic: 33.3 us -> none  [the longest x16 18.3 us: visit_view(): column_xy = jnp.sum(kernel_xy.astype(jnp.float32), axis=1)]
    convert_element_type x17 -> x0, local copies, waits for them, and re-layouts: 29.5 us -> none  [the longest x16 29.4 us: kron_rows(): outer.reshape(outer.shape[:-4] + (rows_xy, rows_xy)).astype(jnp.bfloat16)]
    ppermute x17 -> x0, starting transfers between devices: 26.6 us -> none  [the longest x15 22.3 us: from_behind(): return lax.ppermute(block, axis, route)]
    dynamic_slice x32 -> x0, local copies, waits for them, and re-layouts: 18.8 us -> none  [the longest x16 9.42 us: advance(): back_values[view_id]]
    all_to_all x3 -> x0, starting transfers between devices: 13.7 us -> none  [the longest x1 6.72 us: on_device(): lax.all_to_all(offset_buf, 'view', split_axis=0, concat_axis=0, tiled=True)]
    all_to_all x3 -> x0, waiting for transfers between devices: 12.2 us -> none  [the longest x1 7.45 us: on_device(): lax.all_to_all(data_buf, 'view', split_axis=0, concat_axis=0, tiled=True)]
  transfers between devices with their start and end apart: 20 -> 0, of which waited for: 7 -> 0; matrix products, arithmetic and copies ran while one was open for 71% -> 0% of each run, Pallas kernels for 0% -> 0%
where the time goes in v1:
time: 58.9 us; the launch traced here: 58.6 us
  Pallas kernels  48.1 us (82%)
  local copies, waits for them, and re-layouts  8.45 us (14%)
  other arithmetic  1.33 us (2%)
  between operations  0.76 us (1%)
    pallas_call x1, Pallas kernels, on_device(): pl.pallas_call(functools.partial(kernel, nv, views, bx, by, srows), out_s...  48.1 us
    unnamed x18, local copies, waits for them, and re-layouts  3.71 us
    another operation x5, local copies, waits for them, and re-layouts, facts(): jnp.stack([factor.transpose(0, 2, 1, 3), factor.transpose(0, 3, 1, 2)], a...  2.69 us

profile of v1, /device:TPU:0, one launch (start us, length us, event | category | flops | bytes accessed | tf_op | source)
XLA Modules:
  0.0 58.6 jit_solution(10085005992014954164)
XLA Ops:
  0.6 0.0 copy-start
  0.6 1.1 %copy.42 = bf16[16,16,3,16]{3,2,0,1:T(4,128)(2,1)S(1)} copy(bf16[16,16,3,16]{3,1,2,0:T(8,128)(2,1)} %bitcast.22) | data formatting | bytes 49152 | tf_op jit(solution)/shard_map/stack | solution.py:323
  1.7 0.0 copy-start.2
  1.7 0.0 copy-start.3
  1.8 0.0 copy-start.1
  1.8 0.0 copy-start.4
  1.8 0.0 copy-start.5
  1.8 0.0 copy-start.6
  1.8 0.1 reshape.18
  2.0 1.0 %copy.30 = bf16[16,12,3,12]{3,2,0,1:T(4,128)(2,1)S(1)} copy(bf16[16,12,3,12]{3,0,1,2:T(8,128)(2,1)} %bitcast.24) | data formatting | bytes 27648 | tf_op jit(solution)/shard_map/transpose | solution.py:324
  3.0 0.1 stack.44
  3.1 1.1 %copy.35 = bf16[16,1,16,48]{3,0,2,1:T(8,128)(2,1)S(1)} copy(bf16[16,1,16,48]{2,3,0,1:T(8,128)(2,1)} %bitcast.23) | data formatting | bytes 49152 | tf_op jit(solution)/shard_map/stack | solution.py:323
  4.2 0.0 copy-done
  4.2 0.3 copy.41
  4.5 0.1 fusion.8
  4.6 0.1 pad_maximum_fusion
  4.7 0.8 %copy.36 = bf16[16,2,2,16,84]{4,3,2,1,0:T(8,128)(2,1)} copy(bf16[16,2,2,16,84]{4,0,3,1,2:T(8,128)(2,1)S(1)} %pad_maximum_fusion) | data formatting | bytes 344064 | tf_op jit(solution)/shard_map/stack | solution.py:328
  5.4 0.0 copy-done.2
  5.4 0.1 copy.37
  5.5 0.0 copy-done.3
  5.5 0.1 copy.38
  5.6 0.0 copy-done.1
  5.6 0.1 copy.39
  5.7 0.1 concatenate.5
  5.8 0.6 %convert_element_type.6.meta_ref = f32[16,128]{1,0:T(8,128)} convert(s32[16,128]{1,0:T(8,128)S(1)} %concatenate.5) | non-fusion elementwise | flops 2048 | bytes 16384 | tf_op jit(solution)/shard_map/convert_element_type | solution.py:344
  6.4 0.0 copy-done.4
  6.4 0.7 %copy.40.owner_ref = s32[16,1]{1,0:T(8,128)} copy(s32[16,1]{0,1:T(1,128)S(1)} %copy-done.4) | data formatting | bytes 128 | tf_op args[7]
  7.1 0.0 copy-done.5
  7.1 0.0 copy-done.6
  7.1 0.6 maximum_convert_fusion.scal_ref
  7.6 48.1 %shard_map.131 = (f32[192,128]{1,0:T(8,128)}, f32[64,128]{1,0:T(8,128)}) custom-call(f32[2,16]{1,0:T(2,128)} %maximum_convert_fusion.scal_ref, f32[192,128]{1,0:T(8,128)} %est_ref.1, bf16[16,192,128]{2,1,0:T(8,128)(2,1)} %meas_hbm.1, bf16[16,3,128,128]{3,2,1,0:T(8,128)(2,1)} %kz_hbm.1, bf16[16,64,84]{2,1,0:T(8,128)(2,1)} %bitcast.21, ...), custom_call_target="tpu_custom_call" | custom-call | tf_op jit(solution)/shard_map/pallas_call | solution.py:349
  55.7 1.5 %copy.48 = f32[192,128]{1,0:T(8,128)} copy(f32[192,128]{1,0:T(8,128)} %get-tuple-element.6) | data formatting | bytes 196608
  57.3 1.4 %copy.49 = f32[64,128]{1,0:T(8,128)} copy(f32[64,128]{1,0:T(8,128)} %get-tuple-element.7) | data formatting | bytes 65536
  (2 shorter events, 0.0 us)
Async XLA Ops:
  0.6 3.6 %copy-start = (bf16[16,3,12,12]{3,0,2,1:T(8,128)(2,1)S(1)}, bf16[16,3,12,12]{3,0,2,1:T(8,128)(2,1)}, u32[]{:S(2)}) copy-start(bf16[16,3,12,12]{3,0,2,1:T(8,128)(2,1)} %param.15) | copy-start | bytes 41476
  1.7 3.7 %copy-start.2 = (s32[16]{0:T(128)S(1)}, s32[16]{0:T(128)}, u32[]{:S(2)}) copy-start(s32[16]{0:T(128)} %param.20) | copy-start | bytes 196
  1.7 3.8 %copy-start.3 = (s32[16]{0:T(128)S(1)}, s32[16]{0:T(128)}, u32[]{:S(2)}) copy-start(s32[16]{0:T(128)} %param.21) | copy-start | bytes 196
  1.8 3.8 %copy-start.1 = (s32[16,8]{0,1:T(8,128)S(1)}, s32[16,8]{0,1:T(8,128)}, u32[]{:S(2)}) copy-start(s32[16,8]{0,1:T(8,128)} %param.22) | copy-start | bytes 1540
  1.8 4.6 %copy-start.4 = (s32[16,1]{0,1:T(1,128)S(1)}, s32[16,1]{0,1:T(1,128)}, u32[]{:S(2)}) copy-start(s32[16,1]{0,1:T(1,128)} %param.19) | copy-start | bytes 196
  1.8 5.3 %copy-start.5 = (bf16[16]{0:T(256)(128)(2,1)S(1)}, bf16[16]{0:T(256)(128)(2,1)}, u32[]{:S(2)}) copy-start(bf16[16]{0:T(256)(128)(2,1)} %param.18) | copy-start | bytes 100
  1.8 5.3 %copy-start.6 = (bf16[16]{0:T(256)(128)(2,1)S(1)}, bf16[16]{0:T(256)(128)(2,1)}, u32[]{:S(2)}) copy-start(bf16[16]{0:T(256)(128)(2,1)} %param.17) | copy-start | bytes 100

commit v2 on v1

--- a/solution.py
+++ b/solution.py
@@ -9,6 +9,7 @@
 from jax.sharding import PartitionSpec as P
 
 CAP = 2
+FIELDS = 16
 TROWS = 64
 smooth_rate = 0.24
 
@@ -38,26 +39,32 @@
     bx,
     by,
     srows,
-    scal_ref,
     est_ref,
     meas_hbm,
     kz_hbm,
-    fac_ref,
-    sel_ref,
+    kx_ref,
+    ky_ref,
+    sel_x_ref,
+    sel_y_ref,
+    back_ref,
+    relax_ref,
     owner_ref,
-    meta_ref,
+    source_ref,
+    tile_ref,
+    feather_ref,
     refined_ref,
     smooth_ref,
     rec,
     kz,
-    lanes,
+    lanes_x,
+    lanes_y,
     kron,
+    kron_t,
     logws,
     meta_send,
     meta_recv,
     gather,
     wcol,
-    place,
     data_send,
     data_recv,
     joined_ref,
@@ -75,7 +82,7 @@
     me = lax.axis_index("view")
     rows, depth = est_ref.shape
     rank = kz.shape[1]
-    listed = owner_ref.shape[0]
+    listed = owner_ref.shape[1]
     slab = CAP * srows
     landing = nv * slab
 
@@ -117,70 +124,112 @@
     def data_copy(d):
         return peer_copy(data_send, data_recv, data_send_sem, data_recv_sem, d)
 
-    own_col = owner_ref[...].astype(f32)
-    own_wide = jnp.broadcast_to(own_col, (listed, 128))
+    pl.semaphore_wait(barrier, nv - 1)
+
+    def send_rec(s, c):
+        rec_copy(s).start()
+        return c
+
+    lax.fori_loop(1, views, send_rec, 0)
+
+    spread_x = spread_y = None
+    for r in range(rank):
+        part_x = jnp.dot(kx_ref[r].reshape(bx * views, bx), sel_x_ref[r], preferred_element_type=f32)
+        part_y = jnp.dot(ky_ref[:, r].reshape(views * by, by), sel_y_ref[r], preferred_element_type=f32)
+        spread_x = part_x if spread_x is None else spread_x + part_x
+        spread_y = part_y if spread_y is None else spread_y + part_y
+    lanes_x[...] = spread_x
+    lanes_y[...] = spread_y
+
+    own_row = owner_ref[...].astype(f32)
     if listed < 128:
-        own_wide = jnp.concatenate([own_wide, jnp.full((128 - listed, 128), -1.0, f32)], axis=0)
-    own_row = own_wide.T[0:1, :]
+        own_row = jnp.concatenate([own_row, jnp.full((1, 128 - listed), -1.0, f32)], axis=1)
+    own_wide = jnp.broadcast_to(own_row, (128, 128)).T
     same = (own_wide == own_row).astype(f32)
     ia = lax.broadcasted_iota(jnp.int32, (128, 128), 0)
     ib = lax.broadcasted_iota(jnp.int32, (128, 128), 1)
     earlier = jnp.where(ia < ib, same, 0.0)
     rank_row = jnp.sum(earlier, axis=0, keepdims=True)
     slot_row = own_row * CAP + rank_row
-    slot_of_row = (lax.broadcasted_iota(jnp.int32, (landing, 128), 0) >> 3).astype(f32)
-    pick = (slot_of_row == slot_row).astype(f32)[:, :listed].astype(bf16)
-    meta = jnp.dot(pick, meta_ref[...].astype(bf16), preferred_element_type=f32)
-    meta_send[...] = meta.reshape(nv, slab, 128)
+    fields = jnp.concatenate(
+        [
+            source_ref[...].astype(f32),
+            tile_ref[...].astype(f32),
+            jnp.ones((1, listed), f32),
+            feather_ref[...].astype(f32),
+            jnp.zeros((FIELDS - 3 - srows, listed), f32),
+        ],
+        axis=0,
+    ).astype(bf16)
+    slot_ids = lax.broadcasted_iota(jnp.int32, (nv, 128), 0).astype(f32) * CAP
+    facts = []
+    for c in range(CAP):
+        pick = (slot_ids + c == slot_row).astype(f32)[:, :listed].astype(bf16)
+        facts.append(
+            lax.dot_general(pick, fields, (((1,), (1,)), ((), ())), preferred_element_type=f32)
+        )
+    facts.append(jnp.zeros((nv, 128 - CAP * FIELDS), f32))
+    facts = jnp.concatenate(facts, axis=1)
+    meta_send[...] = facts.reshape(nv, 1, 128)
+
+    def send_meta(d, c):
+        meta_copy(d).start()
+        return c
+
+    lax.fori_loop(1, nv, send_meta, 0)
+
+    row_id = lax.broadcasted_iota(jnp.int32, (landing, 128), 0)
+    lane_of = lax.broadcasted_iota(jnp.int32, (landing, 128), 1)
+    q_of_row = lax.rem(row_id, srows)
+    first_lane = lax.rem(row_id, slab) // srows * FIELDS
+    spread_rows = (
+        lax.broadcasted_iota(jnp.int32, (landing, nv), 0) // slab
+        == lax.broadcasted_iota(jnp.int32, (landing, nv), 1)
+    ).astype(f32).astype(bf16)
+
+    def landing_facts(table, line_lane):
+        wide = jnp.dot(spread_rows, table.astype(bf16), preferred_element_type=f32)
+
+        def column(lane):
+            return jnp.sum(jnp.where(lane_of == lane, wide, 0.0), axis=1, keepdims=True)
+
+        line = column(first_lane + line_lane) + q_of_row[:, 0:1].astype(f32)
+        return line + (column(first_lane + 2) - 1.0) * 4096.0, column(first_lane + 3 + q_of_row)
 
     view0 = lax.rem(me, views)
 
     def expand(view, slot):
-        lanes[...] = jnp.dot(fac_ref[view], sel_ref[...], preferred_element_type=f32)
-        for t in range(2):
-            base = t * 2 * 16
-            y_part = lanes[base + 16 : base + 16 + by, :]
-            for x in range(bx):
-                x_part = lanes[base + x : base + x + 1, :]
-                kron[slot, t, x * by : (x + 1) * by, :] = (x_part * y_part).astype(bf16)
+        y_part = lanes_y[pl.ds(pl.multiple_of(view * by, by), by), :]
+        for x in range(bx):
+            x_part = lanes_x[pl.ds(x * views + view, 1), :]
+            kron[slot, x * by : (x + 1) * by, :] = (x_part * y_part).astype(bf16)
 
     def weigh(view, slot):
-        pieces = []
+        kron_t[slot] = kron[slot].T
+        halves = None
         for r in range(rank):
             column = jnp.sum(kz[view, r].astype(f32), axis=0, keepdims=True)
             hi = column.astype(bf16).astype(f32)
             both = jnp.concatenate([hi, column - hi], axis=1)
-            pieces.append(jnp.broadcast_to(both, (rows, 2 * depth)).astype(bf16))
-        halves = jnp.dot(kron[slot, 1], jnp.concatenate(pieces, axis=0), preferred_element_type=f32)
+            both = jnp.broadcast_to(both, (rows, 2 * depth)).astype(bf16)
+            part = jnp.dot(
+                kron_t[slot, r * rows : (r + 1) * rows, :], both, preferred_element_type=f32
+            )
+            halves = part if halves is None else halves + part
         logws[slot] = jnp.log(halves[:, :depth] + halves[:, depth:])
 
+    def scalar(ref, view):
+        lane = lax.broadcasted_iota(jnp.int32, (1, views), 1)
+        return jnp.sum(jnp.where(lane == view, ref[...].astype(f32), 0.0), axis=1, keepdims=True)
+
     expand(view0, 0)
-    pl.semaphore_wait(barrier, nv - 1)
-
-    def send_rec(s, c):
-        rec_copy(s).start()
-        return c
-
-    lax.fori_loop(1, views, send_rec, 0)
-
-    def send_meta(d, c):
-        meta_copy(d).start()
-        return c
-
-    lax.fori_loop(1, nv, send_meta, 0)
-
     refined_ref[...] = est_ref[...]
     kz_copy.wait()
     weigh(view0, 0)
-    q_of_row = (lax.broadcasted_iota(jnp.int32, (landing, 128), 0) & 7).astype(f32)
-    lane_of = lax.broadcasted_iota(jnp.int32, (landing, 128), 1).astype(f32)
-    valid = meta[:, 2:3]
-    source = meta[:, 0:1] + q_of_row[:, 0:1] + (valid - 1.0) * 4096.0
+    source, weight = landing_facts(facts, 0)
     lane_rows = lax.broadcasted_iota(jnp.int32, (landing, rows), 1).astype(f32)
     gather[...] = (lane_rows == source).astype(f32).astype(bf16)
-    wcol[...] = jnp.broadcast_to(
-        jnp.sum(jnp.where(lane_of == q_of_row + 3.0, meta, 0.0), axis=1, keepdims=True), (landing, depth)
-    )
+    wcol[...] = jnp.broadcast_to(weight, (landing, depth))
     own_rec.wait()
 
     def stop(s, c):
@@ -199,13 +248,18 @@
             ).astype(bf16)
             for r in range(rank)
         ]
-        forward = jnp.dot(kron[slot, 0], jnp.concatenate(along, axis=0), preferred_element_type=f32)
-        ratio = (rec[s].astype(f32) / (forward + scal_ref[0, view])).astype(bf16)
+        forward = jnp.dot(kron[slot], jnp.concatenate(along, axis=0), preferred_element_type=f32)
+        ratio = (rec[s].astype(f32) / (forward + scalar(back_ref, view))).astype(bf16)
         back = [
             jnp.dot(ratio, zeta[r], preferred_element_type=f32).astype(bf16) for r in range(rank)
         ]
-        adjoint = jnp.dot(kron[slot, 1], jnp.concatenate(back, axis=0), preferred_element_type=f32)
-        refined_ref[...] = e * jnp.exp(scal_ref[1, view] * (jnp.log(adjoint) - logws[slot]))
+        adjoint = None
+        for r in range(rank):
+            part = jnp.dot(
+                kron_t[slot, r * rows : (r + 1) * rows, :], back[r], preferred_element_type=f32
+            )
+            adjoint = part if adjoint is None else adjoint + part
+        refined_ref[...] = e * jnp.exp(scalar(relax_ref, view) * (jnp.log(adjoint) - logws[slot]))
         following = lax.rem(view + 1, views)
         expand(following, 1 - slot)
         weigh(following, 1 - slot)
@@ -237,11 +291,9 @@
 
     lax.fori_loop(1, views, done_rec, 0)
 
-    arrived = meta_recv[...].reshape(landing, 128)
-    target = arrived[:, 1:2] + q_of_row[:, 0:1] + (arrived[:, 2:3] - 1.0) * 4096.0
-    place_t = (lane_of == target).astype(f32)
+    target, weights = landing_facts(meta_recv[...].reshape(nv, 128), 1)
+    place_t = (lane_of.astype(f32) == target).astype(f32)
     placed = place_t.T[0:TROWS, :].astype(bf16)
-    weights = jnp.sum(jnp.where(lane_of == q_of_row + 3.0, arrived, 0.0), axis=1, keepdims=True)
     counted = jnp.dot(
         placed, jnp.broadcast_to(weights, (landing, depth)).astype(bf16), preferred_element_type=f32
     )
@@ -317,31 +369,11 @@
     slab = CAP * srows
     landing = nv * slab
 
-    scal = jnp.stack([background.astype(f32), relax.astype(f32)])
-
-    def facts(factor, extent, before, after):
-        both = jnp.stack(
-            [factor.transpose(0, 2, 1, 3), factor.transpose(0, 3, 1, 2)], axis=1
-        ).reshape(views, 2, extent, rank * extent)
-        return jnp.pad(both, ((0, 0), (0, 0), (0, 16 - extent), (before, after)))
-
-    fac = jnp.stack(
-        [facts(kernel_x, bx, 0, rank * by), facts(kernel_y, by, rank * bx, 0)], axis=2
-    ).reshape(views, 64, rank * (bx + by))
     col = np.arange(rank * rows)
     sel_x = col[None, :] // by == np.arange(rank * bx)[:, None]
     sel_y = (col // rows * by + col % by)[None, :] == np.arange(rank * by)[:, None]
-    sel = jnp.asarray(np.concatenate([sel_x, sel_y]).astype(np.float32), bf16)
-    meta = jnp.concatenate(
-        [
-            source_offset[:, None],
-            tile_offset[:, None],
-            jnp.ones((listed, 1), jnp.int32),
-            feather,
-            jnp.zeros((listed, 128 - 3 - srows), jnp.int32),
-        ],
-        axis=1,
-    ).astype(f32)
+    sel_x = jnp.asarray(sel_x.reshape(rank, bx, -1).astype(np.float32), bf16)
+    sel_y = jnp.asarray(sel_y.reshape(rank, by, -1).astype(np.float32), bf16)
 
     vmem = pl.BlockSpec(memory_space=pltpu.VMEM)
     anym = pl.BlockSpec(memory_space=pl.ANY)
@@ -352,28 +384,20 @@
             jax.ShapeDtypeStruct((rows, depth), f32),
             jax.ShapeDtypeStruct((TROWS, depth), f32),
         ),
-        in_specs=[
-            pl.BlockSpec(memory_space=pltpu.SMEM),
-            vmem,
-            anym,
-            anym,
-            vmem,
-            vmem,
-            vmem,
-            vmem,
-        ],
+        in_specs=[vmem, anym, anym] + [vmem] * 10,
         out_specs=(vmem, vmem),
         scratch_shapes=[
             pltpu.VMEM((views, rows, depth), bf16),
             pltpu.VMEM(kernel_z.shape, bf16),
-            pltpu.VMEM((64, rank * rows), f32),
-            pltpu.VMEM((2, 2, rows, rank * rows), bf16),
+            pltpu.VMEM((bx * views, rank * rows), f32),
+            pltpu.VMEM((views * by, rank * rows), f32),
+            pltpu.VMEM((2, rows, rank * rows), bf16),
+            pltpu.VMEM((2, rank * rows, rows), bf16),
             pltpu.VMEM((2, rows, depth), f32),
-            pltpu.VMEM((nv, slab, 128), f32),
-            pltpu.VMEM((nv, slab, 128), f32),
+            pltpu.VMEM((nv, 1, 128), f32),
+            pltpu.VMEM((nv, 1, 128), f32),
             pltpu.VMEM((landing, rows), bf16),
             pltpu.VMEM((landing, depth), f32),
-            pltpu.VMEM((TROWS, landing), bf16),
             pltpu.VMEM((nv, slab, depth), f32),
             pltpu.VMEM((nv, slab, depth), f32),
             pltpu.VMEM((TROWS, depth), f32),
@@ -389,7 +413,21 @@
             dma((2,)),
         ],
         compiler_params=pltpu.CompilerParams(collective_id=0, has_side_effects=True),
-    )(scal, estimate, measured, kernel_z, fac, sel, owner, meta)
+    )(
+        estimate,
+        measured,
+        kernel_z,
+        kernel_x.transpose(1, 2, 0, 3),
+        kernel_y,
+        sel_x,
+        sel_y,
+        background.reshape(1, views),
+        relax.reshape(1, views),
+        owner.reshape(1, listed),
+        source_offset.reshape(1, listed),
+        tile_offset.reshape(1, listed),
+        feather.T,
+    )
 
 
 def solution(mesh):

time: 58.9 us -> 48 us (0.81)
  local copies, waits for them, and re-layouts: 8.45 us -> 2.91 us
  Pallas kernels: 48.1 us -> 44.3 us
  other arithmetic: 1.33 us -> 0 us
    pallas_call x1, Pallas kernels: 48.1 us -> 44.3 us  [on_device(): pl.pallas_call(functools.partial(kernel, nv, views, bx, by, srows), out_s...]
    another operation x7 -> x0, local copies, waits for them, and re-layouts: 3.45 us -> none  [the longest x5 2.69 us: facts(): jnp.stack([factor.transpose(0, 2, 1, 3), factor.transpose(0, 3, 1, 2)], a...]
    transpose x1 -> x0, local copies, waits for them, and re-layouts: 1.04 us -> none  [facts(): factor.transpose(0, 2, 1, 3)]
    unnamed x18 -> x2, local copies, waits for them, and re-layouts: 3.71 us -> 2.91 us
    another operation x3 -> x0, other arithmetic: 0.72 us -> none  [the longest x1 0.55 us: on_device(): scal = jnp.stack([background.astype(f32), relax.astype(f32)])]
    convert_element_type x1 -> x0, other arithmetic: 0.61 us -> none  [on_device(): meta = jnp.concatenate([source_offset[:, None], tile_offset[:, None], jnp...]
where the time goes in v2:
time: 48 us; the launch traced here: 47.8 us
  Pallas kernels  44.3 us (92%)
  local copies, waits for them, and re-layouts  2.91 us (6%)
  between operations  0.64 us (1%)
    pallas_call x1, Pallas kernels, on_device(): pl.pallas_call(functools.partial(kernel, nv, views, bx, by, srows), out_s...  44.3 us
    unnamed x2, local copies, waits for them, and re-layouts  2.91 us

profile of v2, /device:TPU:0, one launch (start us, length us, event | category | flops | bytes accessed | tf_op | source)
XLA Modules:
  0.0 47.8 jit_solution(14785815986236422566)
XLA Ops:
  0.6 44.3 %shard_map.140 = (f32[192,128]{1,0:T(8,128)}, f32[64,128]{1,0:T(8,128)}) custom-call(f32[192,128]{1,0:T(8,128)} %est_ref.1, bf16[16,192,128]{2,1,0:T(8,128)(2,1)} %meas_hbm.1, bf16[16,3,128,128]{3,2,1,0:T(8,128)(2,1)} %kz_hbm.1, bf16[3,12,16,12]{3,2,1,0:T(8,128)(2,1)} %bitcast.7, bf16[16,3,16,16]{3,2,1,0:T(8,128)(2,1)} %ky_ref.1, ...), custom_call_target="tpu_custom_call" | custom-call | tf_op jit(solution)/shard_map/pallas_call | solution.py:381
  44.9 1.5 %copy.17 = f32[192,128]{1,0:T(8,128)} copy(f32[192,128]{1,0:T(8,128)} %get-tuple-element.4) | data formatting | bytes 196608
  46.4 1.4 %copy.18 = f32[64,128]{1,0:T(8,128)} copy(f32[64,128]{1,0:T(8,128)} %get-tuple-element.5) | data formatting | bytes 65536

commit v3 on v2

--- a/solution.py
+++ b/solution.py
@@ -10,6 +10,8 @@
 
 CAP = 2
 FIELDS = 16
+EDGE = 8
+AHEAD = 4
 TROWS = 64
 smooth_rate = 0.24
 
@@ -64,11 +66,10 @@
     meta_send,
     meta_recv,
     gather,
-    wcol,
+    edge_lines,
+    edge_counts,
     data_send,
     data_recv,
-    joined_ref,
-    halo,
     rec_send_sem,
     rec_recv_sem,
     kz_sem,
@@ -76,8 +77,6 @@
     meta_recv_sem,
     data_send_sem,
     data_recv_sem,
-    halo_send_sem,
-    halo_recv_sem,
 ):
     me = lax.axis_index("view")
     rows, depth = est_ref.shape
@@ -130,7 +129,7 @@
         rec_copy(s).start()
         return c
 
-    lax.fori_loop(1, views, send_rec, 0)
+    lax.fori_loop(1, AHEAD, send_rec, 0)
 
     spread_x = spread_y = None
     for r in range(rank):
@@ -227,15 +226,35 @@
     kz_copy.wait()
     weigh(view0, 0)
     source, weight = landing_facts(facts, 0)
+    target, _ = landing_facts(facts, 1)
     lane_rows = lax.broadcasted_iota(jnp.int32, (landing, rows), 1).astype(f32)
-    gather[...] = (lane_rows == source).astype(f32).astype(bf16)
-    wcol[...] = jnp.broadcast_to(weight, (landing, depth))
+    weighted = jnp.where(lane_rows == source, weight, 0.0).astype(bf16)
+    gather[...] = weighted
+    target_row = jnp.broadcast_to(target, (landing, 128)).T[0:1, :]
+    edge_row = lax.broadcasted_iota(jnp.int32, (nv * EDGE, landing), 0)
+    edge_kind = lax.rem(edge_row, EDGE)
+    side = lax.rem(edge_kind, 2)
+    wanted = edge_row // EDGE + 2 * side - 1
+    lane_tile = lax.broadcasted_iota(jnp.int32, (nv * EDGE, landing), 1) // slab
+    near = jnp.where(side == 0, float(TROWS - 1), 0.0)
+    member = ((lane_tile == wanted).astype(f32) * (target_row == near).astype(f32)).astype(bf16)
+    kind = lax.rem(lax.broadcasted_iota(jnp.int32, (nv * EDGE, 1), 0), EDGE)
+    from_lines = jnp.dot(member, weighted, preferred_element_type=f32)
+    edge_lines[...] = jnp.where(kind < 2, from_lines, 0.0).astype(bf16)
+    from_weights = jnp.dot(
+        member, jnp.broadcast_to(weight, (landing, depth)).astype(bf16), preferred_element_type=f32
+    )
+    edge_counts[...] = jnp.where((kind >= 2) & (kind < 4), from_weights, 0.0)
     own_rec.wait()
 
     def stop(s, c):
         @pl.when(s > 0)
         def _():
             rec_copy(s).wait_recv()
+
+        @pl.when(s + AHEAD < views)
+        def _():
+            rec_copy(s + AHEAD).start()
 
         slot = lax.rem(s, 2)
         view = lax.rem(me + s, views)
@@ -267,9 +286,11 @@
 
     lax.fori_loop(0, views, stop, 0)
 
-    refined = refined_ref[...]
-    lines = onehot_dot(gather[...], split3(refined)) * wcol[...]
-    data_send[...] = lines.reshape(nv, slab, depth)
+    parts = split3(refined_ref[...])
+    data_send[:, :slab, :] = onehot_dot(gather[...], parts).reshape(nv, slab, depth)
+    data_send[:, slab:, :] = (onehot_dot(edge_lines[...], parts) + edge_counts[...]).reshape(
+        nv, EDGE, depth
+    )
 
     def send_data(d, c):
         data_copy(d).start()
@@ -303,26 +324,12 @@
         return c
 
     lax.fori_loop(1, nv, take_data, 0)
-    summed = onehot_dot(placed, split3(data_recv[...].reshape(landing, depth)))
+    summed = onehot_dot(placed, split3(data_recv[:, :slab, :].reshape(landing, depth)))
     joined = (1.0 + summed) / (1.0 + counted)
-    joined_ref[...] = joined
-
-    up_copy = pltpu.make_async_remote_copy(
-        src_ref=joined_ref.at[pl.ds(TROWS - 8, 8)],
-        dst_ref=halo.at[0],
-        send_sem=halo_send_sem.at[0],
-        recv_sem=halo_recv_sem.at[0],
-        device_id={"view": lax.rem(me + 1, nv)},
-    )
-    down_copy = pltpu.make_async_remote_copy(
-        src_ref=joined_ref.at[pl.ds(0, 8)],
-        dst_ref=halo.at[1],
-        send_sem=halo_send_sem.at[1],
-        recv_sem=halo_recv_sem.at[1],
-        device_id={"view": lax.rem(me - 1 + nv, nv)},
-    )
-    up_copy.start()
-    down_copy.start()
+    edges = jnp.sum(data_recv[:, slab:, :], axis=0)
+    edges = (1.0 + edges[0:2]) / (1.0 + edges[2:4])
+    low_line = jnp.where(me > 0, edges[0:1], 0.0)
+    high_line = jnp.where(me < nv - 1, edges[1:2], 0.0)
 
     lane = lax.broadcasted_iota(jnp.int32, (TROWS, depth), 1)
     line = lax.broadcasted_iota(jnp.int32, (TROWS, depth), 0)
@@ -336,12 +343,6 @@
     along_depth = flux(right) + flux(left)
     after = pltpu.roll(joined, TROWS - 1, 0)
     before = pltpu.roll(joined, 1, 0)
-    up_copy.wait()
-    down_copy.wait()
-    has_low = (me > 0).astype(f32)
-    has_high = (me < nv - 1).astype(f32)
-    low_line = halo[0, 7:8, :] * has_low
-    high_line = halo[1, 0:1, :] * has_high
     after = jnp.where(line == TROWS - 1, high_line, after)
     before = jnp.where(line == 0, low_line, before)
     smooth_ref[...] = joined + smooth_rate * (flux(after) + flux(before) + along_depth)
@@ -397,11 +398,10 @@
             pltpu.VMEM((nv, 1, 128), f32),
             pltpu.VMEM((nv, 1, 128), f32),
             pltpu.VMEM((landing, rows), bf16),
-            pltpu.VMEM((landing, depth), f32),
-            pltpu.VMEM((nv, slab, depth), f32),
-            pltpu.VMEM((nv, slab, depth), f32),
-            pltpu.VMEM((TROWS, depth), f32),
-            pltpu.VMEM((2, 8, depth), f32),
+            pltpu.VMEM((nv * EDGE, rows), bf16),
+            pltpu.VMEM((nv * EDGE, depth), f32),
+            pltpu.VMEM((nv, slab + EDGE, depth), f32),
+            pltpu.VMEM((nv, slab + EDGE, depth), f32),
             dma((views,)),
             dma((views,)),
             dma,
@@ -409,8 +409,6 @@
             dma((nv,)),
             dma((nv,)),
             dma((nv,)),
-            dma((2,)),
-            dma((2,)),
         ],
         compiler_params=pltpu.CompilerParams(collective_id=0, has_side_effects=True),
     )(

time: 48 us -> 42 us (0.88)
  Pallas kernels: 44.3 us -> 38.2 us
    pallas_call x1, Pallas kernels: 44.3 us -> 38.2 us  [on_device(): pl.pallas_call(functools.partial(kernel, nv, views, bx, by, srows), out_s...]
where the time goes in v3:
time: 42 us; the launch traced here: 41.8 us
  Pallas kernels  38.2 us (91%)
  local copies, waits for them, and re-layouts  2.91 us (7%)
  between operations  0.64 us (2%)
    pallas_call x1, Pallas kernels, on_device(): pl.pallas_call(functools.partial(kernel, nv, views, bx, by, srows), out_s...  38.2 us
    unnamed x2, local copies, waits for them, and re-layouts  2.91 us

profile of v3, /device:TPU:0, one launch (start us, length us, event | category | flops | bytes accessed | tf_op | source)
XLA Modules:
  0.0 41.8 jit_solution(5523903599129459006)
XLA Ops:
  0.6 38.2 %shard_map.140 = (f32[192,128]{1,0:T(8,128)}, f32[64,128]{1,0:T(8,128)}) custom-call(f32[192,128]{1,0:T(8,128)} %est_ref.1, bf16[16,192,128]{2,1,0:T(8,128)(2,1)} %meas_hbm.1, bf16[16,3,128,128]{3,2,1,0:T(8,128)(2,1)} %kz_hbm.1, bf16[3,12,16,12]{3,2,1,0:T(8,128)(2,1)} %bitcast.7, bf16[16,3,16,16]{3,2,1,0:T(8,128)(2,1)} %ky_ref.1, ...), custom_call_target="tpu_custom_call" | custom-call | tf_op jit(solution)/shard_map/pallas_call | solution.py:382
  38.8 1.5 %copy.17 = f32[192,128]{1,0:T(8,128)} copy(f32[192,128]{1,0:T(8,128)} %get-tuple-element.4) | data formatting | bytes 196608
  40.4 1.4 %copy.18 = f32[64,128]{1,0:T(8,128)} copy(f32[64,128]{1,0:T(8,128)} %get-tuple-element.5) | data formatting | bytes 65536

commit v4 on v3

--- a/solution.py
+++ b/solution.py
@@ -382,8 +382,8 @@
     return pl.pallas_call(
         functools.partial(kernel, nv, views, bx, by, srows),
         out_shape=(
-            jax.ShapeDtypeStruct((rows, depth), f32),
-            jax.ShapeDtypeStruct((TROWS, depth), f32),
+            pltpu.VMEM((rows, depth), f32),
+            pltpu.VMEM((TROWS, depth), f32),
         ),
         in_specs=[vmem, anym, anym] + [vmem] * 10,
         out_specs=(vmem, vmem),

time: 42 us -> 39.6 us (0.943)
  local copies, waits for them, and re-layouts: 2.91 us -> 1.26 us
  Pallas kernels: 38.2 us -> 37.6 us
    unnamed x2, local copies, waits for them, and re-layouts: 2.91 us -> 1.26 us
    pallas_call x1, Pallas kernels: 38.2 us -> 37.6 us  [on_device(): pl.pallas_call(functools.partial(kernel, nv, views, bx, by, srows), out_s...]
where the time goes in v4:
time: 39.6 us; the launch traced here: 39.5 us
  Pallas kernels  37.6 us (95%)
  local copies, waits for them, and re-layouts  1.26 us (3%)
  between operations  0.64 us (2%)
    pallas_call x1, Pallas kernels, on_device(): pl.pallas_call(functools.partial(kernel, nv, views, bx, by, srows), out_s...  37.6 us
    unnamed x2, local copies, waits for them, and re-layouts  1.26 us

profile of v4, /device:TPU:0, one launch (start us, length us, event | category | flops | bytes accessed | tf_op | source)
XLA Modules:
  0.0 39.5 jit_solution(17182564422217745042)
XLA Ops:
  0.6 37.6 %shard_map.140 = (f32[192,128]{1,0:T(8,128)S(1)}, f32[64,128]{1,0:T(8,128)S(1)}) custom-call(f32[192,128]{1,0:T(8,128)} %est_ref.1, bf16[16,192,128]{2,1,0:T(8,128)(2,1)} %meas_hbm.1, bf16[16,3,128,128]{3,2,1,0:T(8,128)(2,1)} %kz_hbm.1, bf16[3,12,16,12]{3,2,1,0:T(8,128)(2,1)} %bitcast.7, bf16[16,3,16,16]{3,2,1,0:T(8,128)(2,1)} %ky_ref.1, ...), custom_call_target="tpu_custom_call" | custom-call | tf_op jit(solution)/shard_map/pallas_call | solution.py:382
  38.2 0.6 %copy.17 = f32[192,128]{1,0:T(8,128)} copy(f32[192,128]{1,0:T(8,128)S(1)} %get-tuple-element.2) | data formatting | bytes 196608
  38.9 0.6 %copy.18 = f32[64,128]{1,0:T(8,128)} copy(f32[64,128]{1,0:T(8,128)S(1)} %get-tuple-element.3) | data formatting | bytes 65536
